TPU v7x, 32 devices: a whole 2x2x4 slice. The times are simulated.
32 devices in a mesh: band: 4 (over y, x), ga: 8 (over z, core).
Axes of the slice: x: 2, y: 2, z: 4, core: 2. Of those that a mesh axis runs over, the one named last changes fastest.
Arguments:
- psi: float32 [4096, 4096], P('band', 'ga'), may hold values from -6 to 6
- lower: float32 [4096, 4096], P('band', 'ga'), as said below
Outputs:
- orthonormal: float32 [4096, 4096], P('band', 'ga')
- block_intersection: float32 [4096, 1024], P('band')
Inputs may be any that keep to these rules, and one draw needn't show every extreme that they name: lower is lower triangular with its diagonal between 1 and 2.
All inputs are finite; a program needn't handle non-finite values.
Results may differ from a plain program's by a relative error of at most 0.00022.
Values sent between devices are 32-bit elements; how exact they have to be, the bound alone decides.
A program may use at most 64 MiB of HBM per device.

v0:
```python
import jax
import jax.numpy as jnp
from jax import lax
from jax.sharding import PartitionSpec as P


def from_root(value, axis, source):
    kept = jnp.where(lax.axis_index(axis) == source, value, 0).astype(value.dtype)
    return lax.psum(kept, axis)


def local(psi, lower):
    myblock = lax.axis_index("band")
    sections = lax.axis_size("band")
    nrows = psi.shape[0]
    width = psi.shape[1]
    full_rows = lax.all_gather(lower, "ga", axis=1, tiled=True)
    own_tile = lax.dynamic_slice_in_dim(full_rows, myblock * nrows, nrows, 1)

    def finish(rhs):
        return jax.scipy.linalg.solve_triangular(own_tile, rhs, lower=True)

    def nothing(rhs):
        return jnp.zeros_like(rhs)

    pieces = 1
    span = width // pieces

    def section(section_idx, carry):
        totals, results = carry
        tile = lax.dynamic_slice_in_dim(full_rows, section_idx * nrows, nrows, 1)
        rhs = psi - totals[0]
        ready = lax.cond(myblock == section_idx, finish, nothing, rhs)
        arrived = from_root(ready, "band", section_idx)
        new_results = [jnp.where(myblock == section_idx, ready, results[0])]
        term = jnp.dot(
            tile, arrived, precision=lax.Precision.HIGHEST, preferred_element_type=jnp.float32
        )
        new_totals = [jnp.where(section_idx < myblock, totals[0] + term, totals[0])]
        return (tuple(new_totals), tuple(new_results))

    blank = tuple((jnp.zeros((nrows, span), jnp.float32) for piece in range(pieces)))
    totals, results = lax.fori_loop(0, sections, section, (blank, blank))
    solved = results[0]
    local_intersection = jnp.dot(
        solved, solved.T, precision=lax.Precision.HIGHEST, preferred_element_type=jnp.float32
    )
    intersection = lax.psum(local_intersection, "ga") / (width * lax.axis_size("ga"))
    return (solved, intersection)


def solution(mesh):
    return jax.shard_map(
        local,
        mesh=mesh,
        in_specs=(P("band", "ga"), P("band", "ga")),
        out_specs=(P("band", "ga"), P("band", None)),
        check_vma=False,
    )
```

profile of v0, /device:TPU:0, one launch (start us, length us, event | category | flops | bytes accessed | tf_op | source)
XLA Modules:
  0.0 1144.7 jit_solution(381688450208989229)
XLA Ops:
  7.9 155.5 %all-gather.2.cloned.1.call-done = f32[1024,4096]{1,0:T(8,128)} async-done(((f32[1024,512]{1,0:T(8,128)}), f32[1024,4096]{1,0:T(8,128)}) %all-gather.2.cloned.1.call-update) | async-done | bytes 16777232 | tf_op jit(solution)/shard_map/all_gather | solution.py:17
  163.4 4.8 constant_dynamic-slice_fusion.1
  168.2 857.6 %while.20 = (s32[]{:T(128)}, f32[1024,512]{1,0:T(8,128)}, f32[1024,512]{1,0:T(8,128)}, s32[]{:T(128)}, f32[1024,4096]{1,0:T(8,128)}, /*index=5*/f32[1024,1024]{1...) while((s32[]{:T(128)}, f32[1024,512]{1,0:T(8,128)}, ...), condition=%wide.region_4.5_spmd.clone, body=%wide.region_0.4_spmd.clone.sunk | while | flops 10074390528 | bytes 73794136 | solution.py:43
  168.4 129.2 %conditional.3 = (f32[1024,512]{1,0:T(8,128)}) conditional(s32[]{:T(128)} %convert_element_type.20, () %tuple.91, (f32[1024,1024]{1,0:T(8,128)}, f32[1024,512]{1,0:T(8,128)}, f32[1024,512]{1,0:T(8,128)S(1)}) %tuple.92), branch_computations={%region_1.0_spmd, %region_2.2_spmd} | conditional | flops 3628269568 | bytes 38142244 | solution.py:33
  168.5 4.7 fusion
  173.2 22.5 %while.19 = (s32[]{:T(128)}, f32[1024,1024]{1,0:T(8,128)}, s32[8,2]{0,1:T(2,128)S(1)}, f32[8,128,128]{2,1,0:T(8,128)S(1)}, s32[]{:T(128)}) while((s32[]{:T(128)}, f32[1024,1024]{1,0:T(8,128)}, s32[8,2]{0,1:T(2,128)S(1)}, f32[8,128,128]{2,1,0:T(8,128)S(1)}, s32[]{:T(128)}) %tuple.95), condition=%wide.while_cond, body=%wide.while_body.sunk | while | flops 2 | bytes 131181 | solution.py:21
  173.8 2.2 bitcast_dynamic-update-slice_fusion.2
  176.6 2.2 bitcast_dynamic-update-slice_fusion.2
  179.4 2.2 bitcast_dynamic-update-slice_fusion.2
  182.3 2.2 bitcast_dynamic-update-slice_fusion.2
  185.1 2.2 bitcast_dynamic-update-slice_fusion.2
  187.9 2.2 bitcast_dynamic-update-slice_fusion.2
  190.7 2.2 bitcast_dynamic-update-slice_fusion.2
  193.5 2.1 bitcast_dynamic-update-slice_fusion.2
  195.7 78.6 %custom-call.3 = f32[8,128,128]{1,2,0:T(8,128)S(1)} custom-call(f32[8,128,128]{2,1,0:T(8,128)S(1)} %get-tuple-element.206), custom_call_target="InvertDiagBlocksLowerTriangular" | custom-call | tf_op jit(solution)/shard_map/while/body/eval_jaxpr/cond/branch_1_fun/jit(_solve_triangular)/triangular_solve | solution.py:21
  274.3 2.1 sub.8
  277.5 1.2 convolution_subtract_fusion.3
  279.9 1.3 convolution_subtract_fusion.2
  282.5 1.6 convolution_subtract_fusion.5
  284.0 1.2 constant_dynamic-update-slice_fusion.14
  285.2 1.7 convolution_subtract_fusion.6
  288.1 1.9 convolution_subtract_fusion.1
  291.1 2.0 convolution_subtract_fusion.4
  294.3 2.2 convolution_subtract_fusion
  297.7 4.3 select_select_fusion.2
  302.0 66.0 %all-reduce.5.cloned.1.call-done = f32[1024,512]{1,0:T(8,128)} async-done(((f32[1024,512]{1,0:T(8,128)}), f32[1024,512]{1,0:T(8,128)}) %all-reduce.5.cloned.1.call-update) | async-done | bytes 2097168 | tf_op jit(solution)/shard_map/while/body/eval_jaxpr/psum | solution.py:9
  368.0 10.3 add_select_fusion.2
  378.3 1.8 broadcast_select_fusion.3
  380.1 1.6 conditional.3
  380.1 1.6 broadcast.27
  381.7 4.9 select_select_fusion.2
  386.7 197.2 %all-reduce.5.cloned.1.call-done = f32[1024,512]{1,0:T(8,128)} async-done(((f32[1024,512]{1,0:T(8,128)}), f32[1024,512]{1,0:T(8,128)}) %all-reduce.5.cloned.1.call-update) | async-done | bytes 2097168 | tf_op jit(solution)/shard_map/while/body/eval_jaxpr/psum | solution.py:9
  583.9 10.3 add_select_fusion.2
  594.1 1.8 broadcast_select_fusion.3
  596.0 1.6 conditional.3
  596.0 1.6 broadcast.27
  597.6 4.9 select_select_fusion.2
  602.6 197.1 %all-reduce.5.cloned.1.call-done = f32[1024,512]{1,0:T(8,128)} async-done(((f32[1024,512]{1,0:T(8,128)}), f32[1024,512]{1,0:T(8,128)}) %all-reduce.5.cloned.1.call-update) | async-done | bytes 2097168 | tf_op jit(solution)/shard_map/while/body/eval_jaxpr/psum | solution.py:9
  799.6 10.3 add_select_fusion.2
  809.9 1.8 broadcast_select_fusion.3
  811.7 1.6 conditional.3
  811.8 1.6 broadcast.27
  813.4 4.9 select_select_fusion.2
  818.3 197.2 %all-reduce.5.cloned.1.call-done = f32[1024,512]{1,0:T(8,128)} async-done(((f32[1024,512]{1,0:T(8,128)}), f32[1024,512]{1,0:T(8,128)}) %all-reduce.5.cloned.1.call-update) | async-done | bytes 2097168 | tf_op jit(solution)/shard_map/while/body/eval_jaxpr/psum | solution.py:9
  1015.5 10.3 add_select_fusion.2
  1025.8 10.3 fusion.40
  1036.1 96.6 %all-reduce.3.cloned.1.call-done = f32[1024,1024]{1,0:T(8,128)} async-done(((f32[1024,1024]{1,0:T(8,128)}), f32[1024,1024]{1,0:T(8,128)}) %all-reduce.3.cloned.1.call-update) | async-done | bytes 4194320 | tf_op jit(solution)/shard_map/psum | solution.py:48
  1132.8 5.0 broadcast_multiply_fusion
  (41 shorter events, 14.0 us)
Async XLA Ops:
  7.2 156.3 %all-gather.2.cloned.1.call-start = ((), (), s32[]{:S(2)}) async-start(), calls=%async_computation | async-start | bytes 18874368 | tf_op jit(solution)/shard_map/all_gather | solution.py:17
  168.2 199.8 %all-reduce.5.cloned.1.call-start = ((), (), s32[]{:S(2)}) async-start(), calls=%async_computation.2 | async-start | bytes 4194304 | tf_op jit(solution)/shard_map/while/body/eval_jaxpr/psum | solution.py:9
  378.3 205.6 %all-reduce.5.cloned.1.call-start = ((), (), s32[]{:S(2)}) async-start(), calls=%async_computation.2 | async-start | bytes 4194304 | tf_op jit(solution)/shard_map/while/body/eval_jaxpr/psum | solution.py:9
  594.1 205.5 %all-reduce.5.cloned.1.call-start = ((), (), s32[]{:S(2)}) async-start(), calls=%async_computation.2 | async-start | bytes 4194304 | tf_op jit(solution)/shard_map/while/body/eval_jaxpr/psum | solution.py:9
  809.9 205.6 %all-reduce.5.cloned.1.call-start = ((), (), s32[]{:S(2)}) async-start(), calls=%async_computation.2 | async-start | bytes 4194304 | tf_op jit(solution)/shard_map/while/body/eval_jaxpr/psum | solution.py:9
  1025.8 107.0 %all-reduce.3.cloned.1.call-start = ((), (), s32[]{:S(2)}) async-start(), calls=%async_computation.1 | async-start | bytes 8388608 | tf_op jit(solution)/shard_map/psum | solution.py:48
Sparse Core Ops, SparseCore 0:
  9.6 153.7 all-gather.1
  302.1 65.8 all-reduce.4
  386.8 197.0 all-reduce.4
  602.7 196.9 all-reduce.4
  818.4 197.0 all-reduce.4
  1036.3 96.4 all-reduce.2
where the time goes:
time: 1150 us; the launch traced here: 1140 us
  waiting for transfers between devices  910 us (79%)
  other arithmetic  115 us (10%)
  matrix products  72.7 us (6%)
  local copies, waits for them, and re-layouts  32 us (3%)
  between operations  14.1 us (1%)
    psum x4, waiting for transfers between devices, from_root(): return lax.psum(kept, axis)  657 us
    all_gather x1, waiting for transfers between devices, local(): full_rows = lax.all_gather(lower, 'ga', axis=1, tiled=True)  155 us
    psum x1, waiting for transfers between devices, local(): lax.psum(local_intersection, 'ga') / (width * lax.axis_size('ga'))  96.6 us
    another operation x3, other arithmetic, finish(): return jax.scipy.linalg.solve_triangular(own_tile, rhs, lower=True)  83.3 us
    dot_general x4, matrix products, section(): jnp.dot(tile, arrived, precision=lax.Precision.HIGHEST, preferred_element...  41.1 us
    another operation x27, local copies, waits for them, and re-layouts  27.2 us
  transfers between devices with their start and end apart: 6, of which 6 were waited for; matrix products, arithmetic and copies ran while one was open for 0% of the time, Pallas kernels for 0%

commit v1 on v0

--- a/solution.py
+++ b/solution.py
@@ -14,7 +14,8 @@
     sections = lax.axis_size("band")
     nrows = psi.shape[0]
     width = psi.shape[1]
-    full_rows = lax.all_gather(lower, "ga", axis=1, tiled=True)
+    parts = lax.all_gather(lower, "ga", axis=0, tiled=False)
+    full_rows = jnp.concatenate(parts, axis=1)
     own_tile = lax.dynamic_slice_in_dim(full_rows, myblock * nrows, nrows, 1)
 
     def finish(rhs):

time: 1150 us -> 1160 us (level)
  no operation moved by 1% of the time
where the time goes in v1:
time: 1160 us
  waiting for transfers between devices  912 us (79%)
  other arithmetic  115 us (10%)
  matrix products  72.6 us (6%)
  local copies, waits for them, and re-layouts  42.1 us (4%)
  between operations  14.1 us (1%)
    psum x4, waiting for transfers between devices, from_root(): return lax.psum(kept, axis)  659 us
    all_gather x1, waiting for transfers between devices, local(): parts = lax.all_gather(lower, 'ga', axis=0, tiled=False)  155 us
    psum x1, waiting for transfers between devices, local(): lax.psum(local_intersection, 'ga') / (width * lax.axis_size('ga'))  96.6 us
    another operation x3, other arithmetic, finish(): return jax.scipy.linalg.solve_triangular(own_tile, rhs, lower=True)  83.3 us
    dot_general x4, matrix products, section(): jnp.dot(tile, arrived, precision=lax.Precision.HIGHEST, preferred_element...  41.1 us
    another operation x27, local copies, waits for them, and re-layouts  27.9 us
  transfers between devices with their start and end apart: 6, of which 6 were waited for; matrix products, arithmetic and copies ran while one was open for 0% of the time, Pallas kernels for 0%

profile of v1, /device:TPU:0, one launch (start us, length us, event | category | flops | bytes accessed | tf_op | source)
XLA Modules:
  0.0 1156.7 jit_solution(18079830032886293537)
XLA Ops:
  7.9 155.5 %all-gather.3.cloned.1.call-done = f32[8192,512]{1,0:T(8,128)} async-done(((f32[1024,512]{1,0:T(8,128)}), f32[8192,512]{1,0:T(8,128)}) %all-gather.3.cloned.1.call-update) | async-done | bytes 16777232 | tf_op jit(solution)/shard_map/all_gather | solution.py:17
  163.4 7.2 copy.5
  170.6 2.6 constant_dynamic-slice_fusion.1
  173.3 4.4 copy-done
  177.6 860.2 %while.20 = (s32[]{:T(128)}, f32[1024,512]{1,0:T(8,128)}, f32[1024,512]{1,0:T(8,128)}, s32[]{:T(128)}, f32[1024,4096]{1,0:T(8,128)}, /*index=5*/f32[1024,1024]{1...) while((s32[]{:T(128)}, f32[1024,512]{1,0:T(8,128)}, ...), condition=%wide.region_4.5_spmd.clone, body=%wide.region_0.4_spmd.clone.sunk | while | flops 10074390528 | bytes 73794136 | solution.py:44
  177.9 129.9 %conditional.3 = (f32[1024,512]{1,0:T(8,128)}) conditional(s32[]{:T(128)} %convert_element_type.20, () %tuple.91, (f32[1024,1024]{1,0:T(8,128)}, f32[1024,512]{1,0:T(8,128)}, f32[1024,512]{1,0:T(8,128)S(1)}) %tuple.92), branch_computations={%region_1.0_spmd, %region_2.2_spmd} | conditional | flops 3628269568 | bytes 38142244 | solution.py:34
  177.9 4.7 fusion
  182.6 23.2 %while.19 = (s32[]{:T(128)}, f32[1024,1024]{1,0:T(8,128)}, s32[8,2]{0,1:T(2,128)S(1)}, f32[8,128,128]{2,1,0:T(8,128)S(1)}, s32[]{:T(128)}) while((s32[]{:T(128)}, f32[1024,1024]{1,0:T(8,128)}, s32[8,2]{0,1:T(2,128)S(1)}, f32[8,128,128]{2,1,0:T(8,128)S(1)}, s32[]{:T(128)}) %tuple.95), condition=%wide.while_cond, body=%wide.while_body.sunk | while | flops 2 | bytes 131181 | solution.py:22
  183.3 2.2 bitcast_dynamic-update-slice_fusion.2
  186.2 2.2 bitcast_dynamic-update-slice_fusion.2
  189.1 2.2 bitcast_dynamic-update-slice_fusion.2
  192.0 2.2 bitcast_dynamic-update-slice_fusion.2
  194.9 2.2 bitcast_dynamic-update-slice_fusion.2
  197.8 2.2 bitcast_dynamic-update-slice_fusion.2
  200.7 2.2 bitcast_dynamic-update-slice_fusion.2
  203.6 2.2 bitcast_dynamic-update-slice_fusion.2
  205.8 78.6 %custom-call.3 = f32[8,128,128]{1,2,0:T(8,128)S(1)} custom-call(f32[8,128,128]{2,1,0:T(8,128)S(1)} %get-tuple-element.206), custom_call_target="InvertDiagBlocksLowerTriangular" | custom-call | tf_op jit(solution)/shard_map/while/body/eval_jaxpr/cond/branch_1_fun/jit(_solve_triangular)/triangular_solve | solution.py:22
  284.4 2.1 sub.8
  290.0 1.3 convolution_subtract_fusion.2
  292.6 1.6 convolution_subtract_fusion.5
  295.3 1.7 convolution_subtract_fusion.6
  298.2 1.9 convolution_subtract_fusion.1
  301.2 2.0 convolution_subtract_fusion.4
  304.4 2.2 convolution_subtract_fusion
  307.7 4.3 select_select_fusion.2
  312.1 66.0 %all-reduce.5.cloned.1.call-done = f32[1024,512]{1,0:T(8,128)} async-done(((f32[1024,512]{1,0:T(8,128)}), f32[1024,512]{1,0:T(8,128)}) %all-reduce.5.cloned.1.call-update) | async-done | bytes 2097168 | tf_op jit(solution)/shard_map/while/body/eval_jaxpr/psum | solution.py:9
  378.1 10.3 add_select_fusion.2
  388.3 1.8 broadcast_select_fusion.3
  390.1 1.6 conditional.3
  390.2 1.6 broadcast.27
  391.8 4.9 select_select_fusion.2
  396.7 197.9 %all-reduce.5.cloned.1.call-done = f32[1024,512]{1,0:T(8,128)} async-done(((f32[1024,512]{1,0:T(8,128)}), f32[1024,512]{1,0:T(8,128)}) %all-reduce.5.cloned.1.call-update) | async-done | bytes 2097168 | tf_op jit(solution)/shard_map/while/body/eval_jaxpr/psum | solution.py:9
  594.6 10.3 add_select_fusion.2
  604.9 1.8 broadcast_select_fusion.3
  606.7 1.6 conditional.3
  606.7 1.6 broadcast.27
  608.3 4.9 select_select_fusion.2
  613.3 197.7 %all-reduce.5.cloned.1.call-done = f32[1024,512]{1,0:T(8,128)} async-done(((f32[1024,512]{1,0:T(8,128)}), f32[1024,512]{1,0:T(8,128)}) %all-reduce.5.cloned.1.call-update) | async-done | bytes 2097168 | tf_op jit(solution)/shard_map/while/body/eval_jaxpr/psum | solution.py:9
  811.0 10.3 add_select_fusion.2
  821.3 1.8 broadcast_select_fusion.3
  823.1 1.6 conditional.3
  823.1 1.6 broadcast.27
  824.7 4.9 select_select_fusion.2
  829.7 197.8 %all-reduce.5.cloned.1.call-done = f32[1024,512]{1,0:T(8,128)} async-done(((f32[1024,512]{1,0:T(8,128)}), f32[1024,512]{1,0:T(8,128)}) %all-reduce.5.cloned.1.call-update) | async-done | bytes 2097168 | tf_op jit(solution)/shard_map/while/body/eval_jaxpr/psum | solution.py:9
  1027.5 10.3 add_select_fusion.2
  1037.8 10.3 fusion.40
  1048.2 96.6 %all-reduce.3.cloned.1.call-done = f32[1024,1024]{1,0:T(8,128)} async-done(((f32[1024,1024]{1,0:T(8,128)}), f32[1024,1024]{1,0:T(8,128)}) %all-reduce.3.cloned.1.call-update) | async-done | bytes 4194320 | tf_op jit(solution)/shard_map/psum | solution.py:49
  1144.8 5.0 broadcast_multiply_fusion
  (44 shorter events, 16.7 us)
Async XLA Ops:
  7.2 156.2 %all-gather.3.cloned.1.call-start = ((), (), s32[]{:S(2)}) async-start(), calls=%async_computation.1 | async-start | bytes 18874368 | tf_op jit(solution)/shard_map/all_gather | solution.py:17
  170.6 7.0 copy-start
  177.6 200.4 %all-reduce.5.cloned.1.call-start = ((), (), s32[]{:S(2)}) async-start(), calls=%async_computation.2 | async-start | bytes 4194304 | tf_op jit(solution)/shard_map/while/body/eval_jaxpr/psum | solution.py:9
  388.3 206.3 %all-reduce.5.cloned.1.call-start = ((), (), s32[]{:S(2)}) async-start(), calls=%async_computation.2 | async-start | bytes 4194304 | tf_op jit(solution)/shard_map/while/body/eval_jaxpr/psum | solution.py:9
  604.9 206.1 %all-reduce.5.cloned.1.call-start = ((), (), s32[]{:S(2)}) async-start(), calls=%async_computation.2 | async-start | bytes 4194304 | tf_op jit(solution)/shard_map/while/body/eval_jaxpr/psum | solution.py:9
  821.3 206.2 %all-reduce.5.cloned.1.call-start = ((), (), s32[]{:S(2)}) async-start(), calls=%async_computation.2 | async-start | bytes 4194304 | tf_op jit(solution)/shard_map/while/body/eval_jaxpr/psum | solution.py:9
  1037.8 107.0 %all-reduce.3.cloned.1.call-start = ((), (), s32[]{:S(2)}) async-start(), calls=%async_computation | async-start | bytes 8388608 | tf_op jit(solution)/shard_map/psum | solution.py:49
Sparse Core Ops, SparseCore 0:
  9.6 153.7 all-gather.2
  312.2 65.8 all-reduce.4
  396.8 197.7 all-reduce.4
  613.4 197.5 all-reduce.4
  829.8 197.6 all-reduce.4
  1048.3 96.4 all-reduce.2
